TPU v7x, 32 devices: a whole 2x2x4 slice. The times are simulated.
32 devices in a mesh: seq: 8 (over z, x), head: 4 (over y, core).
Axes of the slice: x: 2, y: 2, z: 4, core: 2. Of those that a mesh axis runs over, the one named last changes fastest.
Arguments:
- query: bfloat16 [8192, 4096], P('seq', 'head'), may hold values from -140 to 140
- key: bfloat16 [8192, 512], P('seq'), may hold values from -7 to 7
- value: bfloat16 [8192, 512], P('seq'), may hold values from -6 to 6
- out_grad: bfloat16 [8192, 4096], P('seq', 'head'), may hold values from -6 to 6
- chosen: int32 [32, 16, 4], P('head', 'seq'), may hold values from 0 to 15, as said below
- drop_seed: int32 [32], P('head'), may hold values from 0 to 16777215
Outputs:
- query_grad: float32 [8192, 4096], P('seq', 'head')
- key_grad: float32 [8192, 512], P(('seq', 'head'))
- value_grad: float32 [8192, 512], P(('seq', 'head'))
Inputs may be any that keep to these rules, and one draw needn't show every extreme that they name: `chosen`: for head h and query block b, entry 0 is b; the other entries are distinct blocks before b whose shard lies at most 3 shards of 1024 tokens before the shard of b, or b itself where fewer such blocks exist.
All inputs are finite; a program needn't handle non-finite values.
Results may differ from a plain program's by a relative error of at most 0.014.
Values may be sent and summed in bfloat16 or wider, within the bound.
A program may use at most 128 MiB of HBM per device.

v0:
```python
import math

import jax
import jax.numpy as jnp
from jax import lax
from jax.experimental import pallas as pl
from jax.experimental.pallas import tpu as pltpu
from jax.sharding import PartitionSpec as P

HD = 128
HEADS = 32
KVH = 4
BLK = 512
TOPK = 4
SPAN = 8
SUB = 128

drop_cut = 6554
keep_gain = 1.0 / 0.9
factor = HD ** (-0.5)
exp_scale = factor * math.log2(math.e)


def shifted(array, axis, by):
    size = lax.axis_size(axis)
    pairs = [(i, i + by) for i in range(size) if 0 <= i + by < size]
    return lax.ppermute(array, axis, pairs)


def kept(x):
    x = x ^ lax.shift_right_logical(x, 15)
    x = x * 73244475
    x = x ^ lax.shift_right_logical(x, 13)
    return (x & 65535) >= drop_cut


def dot(a, b):
    return jnp.dot(a, b, preferred_element_type=jnp.float32)


def grads_kernel(local_blocks, window, steps, chosen_ref, seed_ref, place_ref, q_ref, do_ref, key_ref, value_ref,
                 gathered_ref, qg_ref, far_ref, own_ref, s_ref, pg_ref, d_ref, sg_ref, acc_ref, kt_ref, hash_ref, kv_ref,
                 load_sem):
    step = pl.program_id(0)

    @pl.when(step == 0)
    def _():
        col = pl.ds(pl.multiple_of(place_ref[1], HD), HD)
        loads = [
            pltpu.make_async_copy(key_ref.at[:, col], kv_ref.at[0, 0], load_sem.at[0]),
            pltpu.make_async_copy(value_ref.at[:, col], kv_ref.at[0, 1], load_sem.at[1]),
            pltpu.make_async_copy(gathered_ref, kv_ref.at[pl.ds(1, window - 1)], load_sem.at[2]),
        ]
        for load in loads:
            load.start()
        acc_ref[...] = jnp.zeros_like(acc_ref)
        d_ref[0] = jnp.zeros((BLK, BLK), jnp.bfloat16)
        sg_ref[0] = jnp.zeros((BLK, BLK), jnp.bfloat16)
        for load in loads:
            load.wait()
        for slot in range(window):
            kt_ref[slot] = kv_ref[slot, 0].T
        hash_ref[...] = (lax.broadcasted_iota(jnp.int32, (BLK, BLK), 0) * 9973
                         + lax.broadcasted_iota(jnp.int32, (BLK, BLK), 1) * 40503)

    head = step // local_blocks
    block = lax.rem(step, local_blocks)
    shard = place_ref[0]
    own_block = shard * local_blocks + block
    picks = [chosen_ref[step * TOPK + t] for t in range(TOPK)]
    places = []
    live = [None]
    for t in range(TOPK):
        within = pl.multiple_of(lax.rem(picks[t], local_blocks) * BLK, BLK)
        places.append((shard - picks[t] // local_blocks, within))
        if t:
            dead = picks[t] == picks[0]
            for u in range(1, t):
                dead = jnp.logical_or(dead, picks[t] == picks[u])
            live.append(jnp.logical_not(dead))
    seed_base = seed_ref[head] + own_block * BLK * 40503

    q = q_ref[...]
    do = do_ref[...]
    q_t = q.T
    do_t = do.T
    chunks = [(t, c, (c * SUB if t == 0 else 0)) for t in range(TOPK) for c in range(BLK // SUB)]
    corner = (lax.broadcasted_iota(jnp.int32, (SUB, SUB), 0)
              <= lax.broadcasted_iota(jnp.int32, (SUB, SUB), 1))

    peaks = None
    for t in range(TOPK):
        slot, within = places[t]
        tops = []
        for c in range(BLK // SUB):
            lo = c * SUB if t == 0 else 0
            keys = kv_ref[slot, 0, pl.ds(within + c * SUB, SUB), :]
            s = dot(keys, q_t[:, lo:])
            if t == 0:
                edge = jnp.where(corner, s[:, :SUB], -jnp.inf)
                s = edge if lo + SUB == BLK else jnp.concatenate([edge, s[:, SUB:]], axis=1)
            s_ref[t, c * SUB:(c + 1) * SUB, lo:] = s
            top = jnp.max(s, axis=0, keepdims=True)
            if lo:
                top = jnp.concatenate([jnp.full((1, lo), -jnp.inf, jnp.float32), top], axis=1)
            tops.append(top)
        top = jnp.maximum(jnp.maximum(tops[0], tops[1]), jnp.maximum(tops[2], tops[3]))
        if t:
            top = jnp.where(live[t], top, -jnp.inf)
        peaks = top if peaks is None else jnp.maximum(peaks, top)
    peak = peaks * exp_scale

    total = jnp.zeros((1, BLK), jnp.float32)
    delta = jnp.zeros((1, BLK), jnp.float32)
    for t, c, lo in chunks:
        slot, within = places[t]
        rows = slice(c * SUB, (c + 1) * SUB)
        values = kv_ref[slot, 1, pl.ds(within + c * SUB, SUB), :]
        pg = dot(values, do_t[:, lo:])
        base = peak if t == 0 else jnp.where(live[t], peak, 3e38)
        e = jnp.exp2(s_ref[t, rows, lo:] * exp_scale - base[:, lo:])
        keep = kept(hash_ref[rows, lo:] + (seed_base + picks[t] * BLK * 9973))
        d = jnp.where(keep, e, 0.0)
        pg = jnp.where(keep, pg, 0.0)
        s_ref[t, rows, lo:] = e
        pg_ref[t, rows, lo:] = pg
        d_ref[t, rows, lo:] = d.astype(jnp.bfloat16)
        e_sum = jnp.sum(e, axis=0, keepdims=True)
        dp_sum = jnp.sum(e * pg, axis=0, keepdims=True)
        if lo:
            pad = jnp.zeros((1, lo), jnp.float32)
            e_sum = jnp.concatenate([pad, e_sum], axis=1)
            dp_sum = jnp.concatenate([pad, dp_sum], axis=1)
        total = total + e_sum
        delta = delta + dp_sum

    inv = 1.0 / total
    delta = delta * inv
    q_n = (q_t.astype(jnp.float32) * inv).astype(jnp.bfloat16).T
    do_n = (do_t.astype(jnp.float32) * inv).astype(jnp.bfloat16).T
    qg_t = jnp.zeros((HD, BLK), jnp.float32)
    for t in range(TOPK):
        slot, within = places[t]
        for c in range(BLK // SUB):
            lo = c * SUB if t == 0 else 0
            rows = slice(c * SUB, (c + 1) * SUB)
            sg = s_ref[t, rows, lo:] * (pg_ref[t, rows, lo:] - delta[:, lo:])
            sg_ref[t, rows, lo:] = sg.astype(jnp.bfloat16)
        acc_ref[slot, 1, pl.ds(within, BLK), :] += dot(d_ref[t], do_n)
        acc_ref[slot, 0, pl.ds(within, BLK), :] += dot(sg_ref[t], q_n)
        qg_t = qg_t + dot(kt_ref[slot, :, pl.ds(within, BLK)], sg_ref[t])
    qg_ref[...] = (qg_t * (inv * (keep_gain * factor))).T

    @pl.when(step == steps - 1)
    def _():
        for part, scale in ((0, keep_gain * factor), (1, keep_gain)):
            own_ref[part] = acc_ref[0, part] * scale
            for slot in range(1, window):
                far_ref[slot - 1, part] = (acc_ref[slot, part] * scale).astype(jnp.bfloat16)


def block_grads(query, out_grad, key, value, gathered, chosen, drop_seed, place):
    rows = query.shape[0]
    local_heads = query.shape[1] // HD
    local_blocks = rows // BLK
    window = gathered.shape[0] + 1
    steps = local_heads * local_blocks
    tile = pl.BlockSpec((BLK, HD), lambda i, *_: (lax.rem(i, local_blocks), i // local_blocks))
    flops = steps * TOPK * 5 * 2 * BLK * BLK * HD
    kernel = lambda *refs: grads_kernel(local_blocks, window, steps, *refs)
    return pl.pallas_call(
        kernel,
        name="block_grads",
        grid_spec=pltpu.PrefetchScalarGridSpec(
            num_scalar_prefetch=3,
            grid=(steps,),
            in_specs=[tile, tile] + [pl.BlockSpec(memory_space=pl.ANY)] * 3,
            out_specs=[
                tile,
                pl.BlockSpec((window - 1, 2, rows, HD), lambda i, *_: (0, 0, 0, 0)),
                pl.BlockSpec((2, rows, HD), lambda i, *_: (0, 0, 0)),
            ],
            scratch_shapes=[
                pltpu.VMEM((TOPK, BLK, BLK), jnp.float32),
                pltpu.VMEM((TOPK, BLK, BLK), jnp.float32),
                pltpu.VMEM((TOPK, BLK, BLK), jnp.bfloat16),
                pltpu.VMEM((TOPK, BLK, BLK), jnp.bfloat16),
                pltpu.VMEM((window, 2, rows, HD), jnp.float32),
                pltpu.VMEM((window, HD, rows), jnp.bfloat16),
                pltpu.VMEM((BLK, BLK), jnp.int32),
                pltpu.VMEM((window, 2, rows, HD), jnp.bfloat16),
                pltpu.SemaphoreType.DMA((3,)),
            ],
        ),
        out_shape=[
            jax.ShapeDtypeStruct((rows, local_heads * HD), jnp.float32),
            jax.ShapeDtypeStruct((window - 1, 2, rows, HD), jnp.bfloat16),
            jax.ShapeDtypeStruct((2, rows, HD), jnp.float32),
        ],
        compiler_params=pltpu.CompilerParams(vmem_limit_bytes=60 << 20),
        cost_estimate=pl.CostEstimate(flops=flops, bytes_accessed=20 << 20, transcendentals=steps * TOPK * BLK * BLK),
    )(chosen.reshape(-1), drop_seed, place, query, out_grad, key, value, gathered)


CHUNKS = 4


def seq_peer(by):
    size = lax.axis_size("seq")
    return {"seq": lax.rem(lax.axis_index("seq") + by + size, size)}


def meet(peers):
    barrier = pltpu.get_barrier_semaphore()
    for peer in peers:
        pl.semaphore_signal(barrier, inc=1, device_id=peer, device_id_type=pl.DeviceIdType.MESH)
    pl.semaphore_wait(barrier, len(peers))


def remote(src, dst, send, recv, peer):
    return pltpu.make_async_remote_copy(
        src_ref=src, dst_ref=dst, send_sem=send, recv_sem=recv, device_id=peer,
        device_id_type=pl.DeviceIdType.MESH,
    )


def gather_kernel(key_ref, value_ref, far_ref, send_sem, recv_sem):
    shard = lax.axis_index("seq")
    odd = lax.rem(shard, 2)
    col = pl.ds(pl.multiple_of(lax.axis_index("head") * HD, HD), HD)
    half = key_ref.shape[0] // 2
    mate = {"seq": shard + 1 - 2 * odd}
    ahead = seq_peer(2)
    meet([ahead, seq_peer(-2), mate])

    def own(c):
        return (key_ref, value_ref)[c // 2].at[pl.ds(c % 2 * half, half), col]

    def far(k, c):
        return far_ref.at[k, c // 2, pl.ds(c % 2 * half, half), :]

    def own_ahead(c):
        return remote(own(c), far(1, c), send_sem.at[0, c], recv_sem.at[1, c], ahead)

    def own_mate(c):
        return remote(own(c), far(0, c), send_sem.at[1, c], recv_sem.at[0, c], mate)

    def pass_mate(c, k):
        return remote(far(1, c), far(k, c), send_sem.at[2, c], recv_sem.at[k, c], mate)

    def pass_ahead(c):
        return remote(far(0, c), far(2, c), send_sem.at[3, c], recv_sem.at[2, c], ahead)

    for c in range(CHUNKS):
        own_ahead(c).start()

        @pl.when(odd == 0)
        def _():
            own_mate(c).start()

    for c in range(CHUNKS):
        own_ahead(c).wait_recv()

        @pl.when(odd == 0)
        def _():
            pass_mate(c, 2).start()

        @pl.when(odd == 1)
        def _():
            pass_mate(c, 0).start()

        if c:
            @pl.when(odd == 0)
            def _():
                own_mate(c - 1).wait_recv()
                pass_ahead(c - 1).start()

    @pl.when(odd == 0)
    def _():
        own_mate(CHUNKS - 1).wait_recv()
        pass_ahead(CHUNKS - 1).start()
        for c in range(CHUNKS):
            pass_ahead(c).wait_recv()
            own_mate(c).wait_send()
            pass_mate(c, 2).wait_send()
            pass_ahead(c).wait_send()

    @pl.when(odd == 1)
    def _():
        for c in range(CHUNKS):
            own_mate(c).wait_recv()
            pass_ahead(c).wait_recv()
            pass_mate(c, 0).wait_send()

    for c in range(CHUNKS):
        own_ahead(c).wait_send()


def gather(key, value):
    rows = key.shape[0]
    return pl.pallas_call(
        gather_kernel,
        name="gather",
        out_shape=jax.ShapeDtypeStruct((3, 2, rows, HD), jnp.bfloat16),
        in_specs=[pl.BlockSpec(memory_space=pl.ANY)] * 2,
        out_specs=pl.BlockSpec(memory_space=pl.ANY),
        scratch_shapes=[pltpu.SemaphoreType.DMA((4, CHUNKS)), pltpu.SemaphoreType.DMA((3, CHUNKS))],
        compiler_params=pltpu.CompilerParams(collective_id=0, has_side_effects=True),
    )(key, value)


def reduce_kernel(ranks, far_ref, own_ref, kg_ref, vg_ref, in_far, in_near, in_two, in_own, up_near, up_two,
                  in_head, up_head, total, send_sem, recv_sem, head_send, head_recv):
    shard = lax.axis_index("seq")
    rank = lax.axis_index("head")
    odd = lax.rem(shard, 2)
    mate = {"seq": shard + 1 - 2 * odd}
    back = seq_peer(-2)
    others = [{"head": lax.rem(rank + d, ranks)} for d in range(1, ranks)]
    meet([back, seq_peer(2), mate] + others)
    piece = in_near.shape[2]

    def rows(c):
        return pl.ds(c * piece, piece)

    def far_back(c):
        return remote(far_ref.at[2, :, rows(c)], in_far.at[c], send_sem.at[0, c], recv_sem.at[0, c], back)

    def own_mate(c):
        return remote(far_ref.at[0, :, rows(c)], in_own.at[c], send_sem.at[0, c], recv_sem.at[1, c], mate)

    def far_mate(c):
        return remote(far_ref.at[2, :, rows(c)], in_near.at[c], send_sem.at[1, c], recv_sem.at[2, c], mate)

    def near_mate(c):
        return remote(up_near.at[c], in_near.at[c], send_sem.at[1, c], recv_sem.at[2, c], mate)

    def two_back(c):
        return remote(up_two.at[c], in_two.at[c], send_sem.at[2, c], recv_sem.at[3, c], back)

    def to_head(c):
        return remote(up_head.at[c], in_head.at[rank], head_send.at[c], head_recv.at[rank], {"head": c})

    for c in range(ranks):
        @pl.when(odd == 0)
        def _():
            far_back(c).start()

        @pl.when(odd == 1)
        def _():
            far_mate(c).start()

    @pl.when(odd == 1)
    def _():
        for c in range(ranks):
            own_mate(c).start()

    def stage_near(c):
        @pl.when(odd == 0)
        def _():
            far_back(c).wait_recv()
            up_near[c] = (far_ref[0, :, rows(c)].astype(jnp.float32) + in_far[c].astype(jnp.float32)).astype(jnp.bfloat16)
            near_mate(c).start()

    def stage_two(c):
        near_mate(c).wait_recv()
        up_two[c] = (far_ref[1, :, rows(c)].astype(jnp.float32) + in_near[c].astype(jnp.float32)).astype(jnp.bfloat16)
        two_back(c).start()

    def stage_own(c):
        two_back(c).wait_recv()
        total[c] = own_ref[:, rows(c)] + in_two[c].astype(jnp.float32)

        @pl.when(odd == 0)
        def _():
            own_mate(c).wait_recv()
            total[c] += in_own[c].astype(jnp.float32)

        @pl.when(rank == c)
        def _():
            kg_ref[:, c * HD:(c + 1) * HD] = total[c, 0]
            vg_ref[:, c * HD:(c + 1) * HD] = total[c, 1]

        @pl.when(rank != c)
        def _():
            up_head[c] = total[c].astype(jnp.bfloat16)
            to_head(c).start()

    for k in range(ranks + 2):
        if k < ranks:
            stage_near(k)
        if 0 <= k - 1 < ranks:
            stage_two(k - 1)
        if 0 <= k - 2:
            stage_own(k - 2)

    for c in range(ranks):
        @pl.when(rank != c)
        def _():
            remote(up_head.at[c], in_head.at[c], head_send.at[c], head_recv.at[c], {"head": c}).wait_recv()
            kg_ref[:, c * HD:(c + 1) * HD] = in_head[c, 0].astype(jnp.float32)
            vg_ref[:, c * HD:(c + 1) * HD] = in_head[c, 1].astype(jnp.float32)
            to_head(c).wait_send()

        two_back(c).wait_send()

        @pl.when(odd == 0)
        def _():
            far_back(c).wait_send()
            near_mate(c).wait_send()

        @pl.when(odd == 1)
        def _():
            own_mate(c).wait_send()
            far_mate(c).wait_send()


def reduce(far, own):
    ranks = lax.axis_size("head")
    rows = own.shape[1]
    piece = rows // ranks
    part = pltpu.VMEM((ranks, 2, piece, HD), jnp.bfloat16)
    return pl.pallas_call(
        lambda *refs: reduce_kernel(ranks, *refs),
        name="reduce",
        out_shape=[jax.ShapeDtypeStruct((piece, ranks * HD), jnp.float32)] * 2,
        in_specs=[pl.BlockSpec(memory_space=pltpu.VMEM)] * 2,
        out_specs=[pl.BlockSpec(memory_space=pltpu.VMEM)] * 2,
        scratch_shapes=[part] * 8 + [
            pltpu.VMEM((ranks, 2, piece, HD), jnp.float32),
            pltpu.SemaphoreType.DMA((3, ranks)),
            pltpu.SemaphoreType.DMA((4, ranks)),
            pltpu.SemaphoreType.DMA((ranks,)),
            pltpu.SemaphoreType.DMA((ranks,)),
        ],
        compiler_params=pltpu.CompilerParams(collective_id=1, has_side_effects=True, vmem_limit_bytes=32 << 20),
    )(far, own)


def local(query, key, value, out_grad, chosen, drop_seed):
    rows = query.shape[0]
    local_heads = query.shape[1] // HD
    size = lax.axis_size("seq")
    ranks = lax.axis_size("head")
    window = min(SPAN, size // 2)
    kv_col = lax.axis_index("head") * local_heads // (HEADS // KVH) * HD
    place = jnp.stack([lax.axis_index("seq"), kv_col]).astype(jnp.int32)
    paired = window == 4 and ranks == KVH and size % 2 == 0
    if paired:
        gathered = gather(key, value)
    else:
        own_pair = jnp.stack(
            [
                lax.dynamic_slice_in_dim(key, kv_col, HD, 1),
                lax.dynamic_slice_in_dim(value, kv_col, HD, 1),
            ]
        )
        gathered = jnp.stack([shifted(own_pair, "seq", d) for d in range(1, window)])
    query_grad, far, own = block_grads(query, out_grad, key, value, gathered, chosen, drop_seed, place)
    if paired:
        key_grad, value_grad = reduce(far, own)
        return (query_grad, key_grad, value_grad)
    for d in range(1, window):
        own = own + shifted(far[d - 1], "seq", -d).astype(jnp.float32)
    pieces = own.reshape(2, ranks, rows // ranks, HD)
    swapped = lax.all_to_all(pieces, "head", 1, 1, tiled=True)
    summed = swapped.reshape(2, KVH, ranks // KVH, rows // ranks, HD).sum(2)
    both = summed.transpose(0, 2, 1, 3).reshape(2, rows // ranks, KVH * HD)
    return (query_grad, both[0], both[1])


def solution(mesh):
    in_specs = (
        P("seq", "head"),
        P("seq", None),
        P("seq", None),
        P("seq", "head"),
        P("head", "seq", None),
        P("head"),
    )
    out_specs = (P("seq", "head"), P(("seq", "head"), None), P(("seq", "head"), None))
    return jax.shard_map(local, mesh=mesh, in_specs=in_specs, out_specs=out_specs, check_vma=False)
```

profile of v0, /device:TPU:23, one launch (start us, length us, event | category | flops | bytes accessed | tf_op | source)
XLA Modules:
  0.0 155.9 jit_solution(9537788473426179216)
XLA Ops:
  0.6 0.6 pad_add_fusion.refs_2_
  1.2 0.8 copy.10
  2.0 0.6 reshape.9.refs_0_
  2.6 24.7 %gather.1.refs_7_ = bf16[3,2,1024,128]{3,2,1,0:T(8,128)(2,1)} custom-call(bf16[1024,512]{1,0:T(8,128)(2,1)} %refs_5_.1, bf16[1024,512]{1,0:T(8,128)(2,1)} %refs_6_.1), custom_call_target="tpu_custom_call" | custom-call | tf_op jit(solution)/shard_map/gather/pallas_call | solution.py:301
  27.4 91.1 %block_grads.1 = (f32[1024,1024]{1,0:T(8,128)}, bf16[3,2,1024,128]{3,2,1,0:T(8,128)(2,1)}, f32[2,1024,128]{2,1,0:T(8,128)}) custom-call(s32[64]{0:T(128)} %reshape.9.refs_0_, s32[8]{0:T(128)} %refs_1_.1, s32[2]{0:T(128)} %pad_add_fusion.refs_2_, bf16[1024,1024]{1,0:T(8,128)(2,1)} %refs_3_.1, bf16[1024,1024]{1,0:T(8,128)(2,1)} %refs_4_.1, ...), custom_call_target="tpu_custom_call" | custom-call | flops 21474836480 | bytes 20971520 | tf_op jit(solution)/shard_map/block_grads/pallas_call | solution.py:171
  118.5 0.0 copy-start
  118.5 1.4 copy-done
  119.9 0.0 copy-start.1
  119.9 1.2 copy-done.1
  121.1 33.2 %reduce.1 = (f32[256,512]{1,0:T(8,128)S(1)}, f32[256,512]{1,0:T(8,128)S(1)}) custom-call(bf16[3,2,1024,128]{3,2,1,0:T(8,128)(2,1)S(1)} %copy-done, f32[2,1024,128]{2,1,0:T(8,128)S(1)} %copy-done.1), custom_call_target="tpu_custom_call" | custom-call | tf_op jit(solution)/shard_map/reduce/pallas_call | solution.py:423
  154.3 0.8 copy.13
  155.1 0.8 copy.14
Async XLA Ops:
  118.5 1.4 copy-start
  119.9 1.2 copy-start.1
where the time goes:
time: 157 us; the launch traced here: 156 us
  Pallas kernels  149 us (95%)
  local copies, waits for them, and re-layouts  5.59 us (4%)
    pallas_call x1, Pallas kernels, block_grads(): pl.pallas_call(kernel, name='block_grads', grid_spec=pltpu.PrefetchScalar...  91.1 us
    pallas_call x1, Pallas kernels, reduce(): pl.pallas_call(lambda *refs: reduce_kernel(ranks, *refs), name='reduce',...  33.2 us
    pallas_call x1, Pallas kernels, gather(): pl.pallas_call(gather_kernel, name='gather', out_shape=jax.ShapeDtypeStru...  24.7 us
    unnamed x7, local copies, waits for them, and re-layouts  4.99 us

commit v1 on v0

v1 whole, which is shorter than its diff:
```python
import math

import jax
import jax.numpy as jnp
from jax import lax
from jax.experimental import pallas as pl
from jax.experimental.pallas import tpu as pltpu
from jax.sharding import PartitionSpec as P

HD = 128
HEADS = 32
KVH = 4
BLK = 512
TOPK = 4
SPAN = 8
SUB = 128
ROWS = 16

drop_cut = 6554
keep_gain = 1.0 / 0.9
factor = HD ** (-0.5)
exp_scale = factor * math.log2(math.e)


def shifted(array, axis, by):
    size = lax.axis_size(axis)
    pairs = [(i, i + by) for i in range(size) if 0 <= i + by < size]
    return lax.ppermute(array, axis, pairs)


def kept(x):
    x = x ^ lax.shift_right_logical(x, 15)
    x = x * 73244475
    x = x ^ lax.shift_right_logical(x, 13)
    return (x & 65535) >= drop_cut


def dot(a, b):
    return jnp.dot(a, b, preferred_element_type=jnp.float32)


def grads_kernel(local_blocks, window, steps, chosen_ref, seed_ref, q_hbm, do_hbm, key_ref, value_ref, gathered_ref,
                 bits_hbm, qg_ref, far_ref, own_ref, s0, s1, g0, g1, d0, d1, sg0, sg1, mx0, mx1, qt0, qt1, dt0, dt1,
                 qn0, qn1, dn0, dn1, inv0, inv1, out0, out1, acc_ref, kt_ref, kv_ref, bits_ref, q_ref, do_ref,
                 load_sem, out_sem):
    S, G, D, SG = (s0, s1), (g0, g1), (d0, d1), (sg0, sg1)
    MX, QT, DT = (mx0, mx1), (qt0, qt1), (dt0, dt1)
    QN, DN, INV, OUT = (qn0, qn1), (dn0, dn1), (inv0, inv1), (out0, out1)
    pair = pl.program_id(0)
    shard = lax.axis_index("seq")
    corner = (lax.broadcasted_iota(jnp.int32, (SUB, SUB), 0)
              <= lax.broadcasted_iota(jnp.int32, (SUB, SUB), 1))

    def picks_of(item):
        return [chosen_ref[item * TOPK + t] for t in range(TOPK)]

    def place(pick):
        return shard - pick // local_blocks, pl.multiple_of(lax.rem(pick, local_blocks) * BLK, BLK)

    def where_of(item):
        head = item // local_blocks
        return (pl.ds(pl.multiple_of(lax.rem(item, local_blocks) * BLK, BLK), BLK),
                pl.ds(pl.multiple_of(head * HD, HD), HD))

    def low(t, row):
        return row // SUB * SUB if t == 0 else 0

    def score_parts(item, p):
        places = [place(pick) for pick in picks_of(item)]

        def turn():
            rows, cols = where_of(item)
            QT[p][...] = q_ref[rows, cols].T
            DT[p][...] = do_ref[rows, cols].T

        def scores(t, row, size):
            slot, within = places[t]
            lo = low(t, row)
            keys = kv_ref[slot, 0, pl.ds(within + row, size), :]
            s = dot(keys, QT[p][:, lo:])
            if t == 0:
                edge = jnp.where(corner, s[:, :SUB], -jnp.inf)
                s = edge if lo + SUB == BLK else jnp.concatenate([edge, s[:, SUB:]], axis=1)
            S[p][t * BLK + row:t * BLK + row + size, lo:] = s
            top = jnp.max(s.reshape(size // 8, 8, BLK - lo), axis=0)
            if row:
                top = jnp.maximum(MX[p][t, :, lo:], top)
            MX[p][t, :, lo:] = top

        def pulls(t, row, size):
            slot, within = places[t]
            lo = low(t, row)
            values = kv_ref[slot, 1, pl.ds(within + row, size), :]
            G[p][t * BLK + row:t * BLK + row + size, lo:] = dot(values, DT[p][:, lo:])

        parts = [turn]
        for t in range(TOPK):
            size = SUB if t == 0 else 2 * SUB
            for row in range(0, BLK, size):
                parts.append(lambda t=t, row=row, size=size: scores(t, row, size))
                parts.append(lambda t=t, row=row, size=size: pulls(t, row, size))
        return parts

    def soft_parts(item, p):
        picks = picks_of(item)
        live = [None]
        for t in range(1, TOPK):
            dead = picks[t] == picks[0]
            for u in range(1, t):
                dead = jnp.logical_or(dead, picks[t] == picks[u])
            live.append(jnp.logical_not(dead))
        st = {}

        def head():
            tops = MX[p][0]
            for t in range(1, TOPK):
                tops = jnp.maximum(tops, jnp.where(live[t], MX[p][t], -jnp.inf))
            peak = jnp.max(tops, axis=0, keepdims=True) * exp_scale
            st["base"] = [peak] + [jnp.where(live[t], peak, 3e38) for t in range(1, TOPK)]
            st["total"] = jnp.zeros((8, BLK), jnp.float32)
            st["delta"] = jnp.zeros((8, BLK), jnp.float32)

        word = item * TOPK // 32

        def weigh(t, row):
            lo = low(t, row)
            at = (slice(t * BLK + row, t * BLK + row + ROWS), slice(lo, BLK))
            bit = lax.shift_left(jnp.int32(1), lax.rem(item * TOPK, 32) + t)
            keep = (bits_ref[word, row:row + ROWS, lo:] & bit) != 0
            e = jnp.exp2(S[p][at] * exp_scale - st["base"][t][:, lo:])
            d = jnp.where(keep, e, 0.0)
            dp = d * G[p][at]
            S[p][at] = e
            G[p][at] = dp
            D[p][at] = d.astype(jnp.bfloat16)
            wide = BLK - lo
            e_sum = jnp.sum(e.reshape(ROWS // 8, 8, wide), axis=0)
            dp_sum = jnp.sum(dp.reshape(ROWS // 8, 8, wide), axis=0)
            if lo:
                pad = lambda old, add: jnp.concatenate([old[:, :lo], old[:, lo:] + add], axis=1)
            else:
                pad = lambda old, add: old + add
            st["total"] = pad(st["total"], e_sum)
            st["delta"] = pad(st["delta"], dp_sum)

        def middle():
            inv = 1.0 / jnp.sum(st["total"], axis=0, keepdims=True)
            st["mean"] = jnp.sum(st["delta"], axis=0, keepdims=True) * inv
            INV[p][...] = inv
            QN[p][...] = (QT[p][...].astype(jnp.float32) * inv).astype(jnp.bfloat16)
            DN[p][...] = (DT[p][...].astype(jnp.float32) * inv).astype(jnp.bfloat16)

        def slope(t, row):
            lo = low(t, row)
            at = (slice(t * BLK + row, t * BLK + row + ROWS), slice(lo, BLK))
            SG[p][at] = (G[p][at] - S[p][at] * st["mean"][:, lo:]).astype(jnp.bfloat16)

        parts = [(1, head)]
        spots = [(t, row) for t in range(TOPK) for row in range(0, BLK, ROWS)]
        for t, row in spots:
            parts.append((3, lambda t=t, row=row: weigh(t, row)))
        parts.append((1, middle))
        for t, row in spots:
            parts.append((1, lambda t=t, row=row: slope(t, row)))
        return parts

    def grad_parts(item, p):
        places = [place(pick) for pick in picks_of(item)]

        def keyed(t, part):
            slot, within = places[t]
            left, right = ((QN, SG), (DN, D))[part]
            add = lax.dot_general(left[p][...], right[p][t * BLK:(t + 1) * BLK, :], (((1,), (1,)), ((), ())),
                                  preferred_element_type=jnp.float32)
            acc_ref[slot, part, :, pl.ds(within, BLK)] += add

        def queried(lo, size):
            keys_t = jnp.concatenate([kt_ref[slot, :, pl.ds(within, BLK)] for slot, within in places], axis=1)
            part = dot(keys_t, SG[p][:, lo:lo + size])
            OUT[p][lo:lo + size, :] = (part * (INV[p][:, lo:lo + size] * (keep_gain * factor))).T

        parts = []
        for t in range(TOPK):
            parts.append(lambda t=t: keyed(t, 1))
            parts.append(lambda t=t: keyed(t, 0))
            if t % 2:
                parts.append(lambda t=t: queried(t // 2 * 2 * SUB, 2 * SUB))
        return parts

    def run(parts):
        for part in parts:
            part()

    def mix(soft, dots):
        whole = sum(cost for cost, _ in soft)
        done, k = 0, 0
        for cost, part in soft:
            while k < len(dots) and k * whole <= done * len(dots):
                dots[k]()
                k += 1
            part()
            done += cost
        run(dots[k:])

    def weave(a, b):
        spots = [((i + 0.5) / len(a), 0, x) for i, x in enumerate(a)]
        spots += [((i + 0.5) / len(b), 1, x) for i, x in enumerate(b)]
        return [x for _, _, x in sorted(spots, key=lambda y: y[:2])]

    def send(item, p):
        rows, cols = where_of(item)
        return pltpu.make_async_copy(OUT[p], qg_ref.at[rows, cols], out_sem.at[p])

    @pl.when(pair == 0)
    def _():
        kv_col = pl.ds(pl.multiple_of(kv_column(), HD), HD)
        loads = [
            pltpu.make_async_copy(q_hbm, q_ref, load_sem.at[0]),
            pltpu.make_async_copy(do_hbm, do_ref, load_sem.at[1]),
            pltpu.make_async_copy(key_ref.at[:, kv_col], kv_ref.at[0, 0], load_sem.at[2]),
            pltpu.make_async_copy(value_ref.at[:, kv_col], kv_ref.at[0, 1], load_sem.at[3]),
            pltpu.make_async_copy(gathered_ref, kv_ref.at[pl.ds(1, window - 1)], load_sem.at[4]),
            pltpu.make_async_copy(bits_hbm, bits_ref, load_sem.at[5]),
        ]
        for load in loads:
            load.start()
        acc_ref[...] = jnp.zeros_like(acc_ref)
        for ref in D + SG:
            ref[...] = jnp.zeros_like(ref)
        QN[1][...] = jnp.zeros_like(QN[1])
        DN[1][...] = jnp.zeros_like(DN[1])
        INV[1][...] = jnp.zeros_like(INV[1])
        for load in loads:
            load.wait()
        for slot in range(window):
            kt_ref[slot] = kv_ref[slot, 0].T
        run(score_parts(0, 0))

    last = pl.num_programs(0) - 1
    for p in range(2):
        item = pair * 2 + p
        after = jnp.minimum(item + 1, steps - 1)
        before = jnp.maximum(item - 1, 0)
        target = jnp.where(item == 0, 1, item - 1)

        @pl.when(pair > 0)
        def _():
            send(jnp.maximum(target - 2, 0), 1 - p).wait()

        if p == 1:
            pass
        mix(soft_parts(item, p), weave(score_parts(after, 1 - p), grad_parts(before, 1 - p)))
        send(target, 1 - p).start()

    @pl.when(pair == last)
    def _():
        send(0, 1).wait()
        run(grad_parts(steps - 1, 1))
        send(steps - 1, 1).start()
        for part, scale in ((0, keep_gain * factor), (1, keep_gain)):
            own_ref[part] = acc_ref[0, part] * scale
            for slot in range(1, window):
                far_ref[slot - 1, part] = (acc_ref[slot, part] * scale).astype(jnp.bfloat16)
        send(0, 0).wait()
        send(0, 1).wait()


def kv_column():
    return lax.axis_index("head") * (HEADS // lax.axis_size("head")) // (HEADS // KVH) * HD


def block_grads(query, out_grad, key, value, gathered, bits, chosen, drop_seed):
    rows = query.shape[0]
    local_heads = query.shape[1] // HD
    local_blocks = rows // BLK
    window = gathered.shape[0] + 1
    steps = local_heads * local_blocks
    flops = steps * TOPK * 5 * 2 * BLK * BLK * HD
    kernel = lambda *refs: grads_kernel(local_blocks, window, steps, *refs)
    f32, bf16 = jnp.float32, jnp.bfloat16
    twice = lambda shape, dtype: [pltpu.VMEM(shape, dtype)] * 2
    return pl.pallas_call(
        kernel,
        name="block_grads",
        grid_spec=pltpu.PrefetchScalarGridSpec(
            num_scalar_prefetch=2,
            grid=(steps // 2,),
            in_specs=[pl.BlockSpec(memory_space=pl.ANY)] * 6,
            out_specs=[
                pl.BlockSpec(memory_space=pl.ANY),
                pl.BlockSpec((window - 1, 2, HD, rows), lambda i, *_: (0, 0, 0, 0)),
                pl.BlockSpec((2, HD, rows), lambda i, *_: (0, 0, 0)),
            ],
            scratch_shapes=twice((TOPK * BLK, BLK), f32) + twice((TOPK * BLK, BLK), f32)
            + twice((TOPK * BLK, BLK), bf16) + twice((TOPK * BLK, BLK), bf16)
            + twice((TOPK, 8, BLK), f32)
            + twice((HD, BLK), bf16) * 4
            + twice((1, BLK), f32) + twice((BLK, HD), f32)
            + [
                pltpu.VMEM((window, 2, HD, rows), f32),
                pltpu.VMEM((window, HD, rows), bf16),
                pltpu.VMEM((window, 2, rows, HD), bf16),
                pltpu.VMEM(bits.shape, jnp.int32),
                pltpu.VMEM(query.shape, bf16),
                pltpu.VMEM(query.shape, bf16),
                pltpu.SemaphoreType.DMA((6,)),
                pltpu.SemaphoreType.DMA((2,)),
            ],
        ),
        out_shape=[
            jax.ShapeDtypeStruct((rows, local_heads * HD), f32),
            jax.ShapeDtypeStruct((window - 1, 2, HD, rows), bf16),
            jax.ShapeDtypeStruct((2, HD, rows), f32),
        ],
        compiler_params=pltpu.CompilerParams(vmem_limit_bytes=60 << 20),
        cost_estimate=pl.CostEstimate(flops=flops, bytes_accessed=20 << 20, transcendentals=steps * TOPK * BLK * BLK),
    )(chosen.reshape(-1), drop_seed, query, out_grad, key, value, gathered, bits)


def mask_rows(chosen_ref, seed_ref, bits_ref, steps, local_blocks, row, lo):
    shard = lax.axis_index("seq")
    size = 16
    at = (pl.ds(row, size), slice(0, BLK))
    place = ((lax.broadcasted_iota(jnp.int32, (size, BLK), 0) + row) * 9973
             + lax.broadcasted_iota(jnp.int32, (size, BLK), 1) * 40503)
    for word in range(bits_ref.shape[0]):
        held = jnp.zeros((size, BLK), jnp.int32)
        for j in range(32):
            item, t = (word * 32 + j) // TOPK, j % TOPK
            own = shard * local_blocks + item % local_blocks
            base = seed_ref[item // local_blocks] + own * (BLK * 40503) + chosen_ref[item * TOPK + t] * (BLK * 9973)
            cut = lo if t == 0 else 0
            bit = jnp.int32(1 << j if j < 31 else -(1 << 31))
            part = jnp.where(kept(place[:, cut:] + base), bit, 0)
            if cut:
                part = jnp.concatenate([jnp.zeros((size, cut), jnp.int32), part], axis=1)
            held = held | part
        bits_ref[(word,) + at] = held


def masks_kernel(steps, local_blocks, chosen_ref, seed_ref, bits_ref):
    @pl.loop(0, BLK // 16)
    def _(i):
        mask_rows(chosen_ref, seed_ref, bits_ref, steps, local_blocks, pl.multiple_of(i * 16, 16), 0)


def masks(chosen, drop_seed, local_blocks):
    steps = chosen.size // TOPK
    smem = pl.BlockSpec(memory_space=pltpu.SMEM)
    return pl.pallas_call(
        lambda *refs: masks_kernel(steps, local_blocks, *refs),
        name="masks",
        out_shape=jax.ShapeDtypeStruct((steps * TOPK // 32, BLK, BLK), jnp.int32),
        in_specs=[smem, smem],
        out_specs=pl.BlockSpec(memory_space=pltpu.VMEM),
    )(chosen.reshape(-1), drop_seed)


CHUNKS = 4


def seq_peer(by):
    size = lax.axis_size("seq")
    return {"seq": lax.rem(lax.axis_index("seq") + by + size, size)}


def meet(peers):
    barrier = pltpu.get_barrier_semaphore()
    for peer in peers:
        pl.semaphore_signal(barrier, inc=1, device_id=peer, device_id_type=pl.DeviceIdType.MESH)
    pl.semaphore_wait(barrier, len(peers))


def remote(src, dst, send, recv, peer):
    return pltpu.make_async_remote_copy(
        src_ref=src, dst_ref=dst, send_sem=send, recv_sem=recv, device_id=peer,
        device_id_type=pl.DeviceIdType.MESH,
    )


def gather_kernel(steps, local_blocks, chosen_ref, seed_ref, key_ref, value_ref, far_ref, bits_ref, send_sem, recv_sem):
    shard = lax.axis_index("seq")
    size = lax.axis_size("seq")
    odd = lax.rem(shard, 2)
    col = pl.ds(pl.multiple_of(lax.axis_index("head") * HD, HD), HD)
    half = key_ref.shape[0] // 2
    mate = {"seq": shard + 1 - 2 * odd}
    ahead = seq_peer(2)
    barrier = pltpu.get_barrier_semaphore()
    gives = shard < size - 2
    takes = shard >= 2
    relays = jnp.logical_and(odd == 0, jnp.logical_and(gives, takes))
    relayed = jnp.logical_and(odd == 0, shard >= 4)

    def greet(peer):
        pl.semaphore_signal(barrier, inc=1, device_id=peer, device_id_type=pl.DeviceIdType.MESH)

    for peer in (ahead, seq_peer(-2), mate):
        greet(peer)
    pl.semaphore_wait(barrier, 3)

    def own(c):
        return (key_ref, value_ref)[c // 2].at[pl.ds(c % 2 * half, half), col]

    def far(k, c):
        return far_ref.at[k, c // 2, pl.ds(c % 2 * half, half), :]

    def own_ahead(c):
        return remote(own(c), far(1, c), send_sem.at[0, c], recv_sem.at[1, c], ahead)

    def own_mate(c):
        return remote(own(c), far(0, c), send_sem.at[1, c], recv_sem.at[0, c], mate)

    def pass_mate(c, k):
        return remote(far(1, c), far(k, c), send_sem.at[2, c], recv_sem.at[k, c], mate)

    def pass_ahead(c):
        return remote(far(0, c), far(2, c), send_sem.at[3, c], recv_sem.at[2, c], ahead)

    for c in range(CHUNKS):
        @pl.when(gives)
        def _():
            own_ahead(c).start()

        @pl.when(odd == 0)
        def _():
            own_mate(c).start()

    def near_event(c):
        @pl.when(takes)
        def _():
            own_ahead(c).wait_recv()

            @pl.when(odd == 0)
            def _():
                pass_mate(c, 2).start()

            @pl.when(odd == 1)
            def _():
                pass_mate(c, 0).start()

    def far_event(c):
        @pl.when(relays)
        def _():
            own_mate(c).wait_recv()
            pass_ahead(c).start()

    events = [lambda c=c: near_event(c) for c in range(CHUNKS)] + [lambda c=c: far_event(c) for c in range(CHUNKS)]
    order = [0, 1, 4, 2, 5, 3, 6, 7]
    spots = MASK_SPOTS
    rows = 16
    loops = SUB // rows
    for c in range(BLK // SUB):
        @pl.loop(0, loops)
        def _(i):
            for spot, event in zip(spots, order):
                if spot // loops == c:
                    pl.when(i == spot % loops)(events[event])
            mask_rows(chosen_ref, seed_ref, bits_ref, steps, local_blocks,
                      pl.multiple_of(c * SUB + i * rows, rows), c * SUB)

    for c in range(CHUNKS):
        @pl.when(jnp.logical_and(odd == 0, takes))
        def _():
            pass_mate(c, 2).wait_send()

        @pl.when(jnp.logical_and(odd == 0, jnp.logical_and(takes, jnp.logical_not(gives))))
        def _():
            own_mate(c).wait_recv()

        @pl.when(odd == 0)
        def _():
            own_mate(c).wait_send()

        @pl.when(relayed)
        def _():
            pass_ahead(c).wait_recv()

        @pl.when(relays)
        def _():
            pass_ahead(c).wait_send()

        @pl.when(odd == 1)
        def _():
            own_mate(c).wait_recv()

        @pl.when(jnp.logical_and(odd == 1, takes))
        def _():
            remote(far(1, c), far(2, c), send_sem.at[2, c], recv_sem.at[2, c], mate).wait_recv()
            pass_mate(c, 0).wait_send()

        @pl.when(gives)
        def _():
            own_ahead(c).wait_send()


MASK_SPOTS = [11, 14, 15, 18, 19, 22, 23, 27]


def gather(key, value, chosen, drop_seed):
    rows = key.shape[0]
    steps = chosen.size // TOPK
    smem = pl.BlockSpec(memory_space=pltpu.SMEM)
    return pl.pallas_call(
        lambda *refs: gather_kernel(steps, rows // BLK, *refs),
        name="gather",
        out_shape=[
            jax.ShapeDtypeStruct((3, 2, rows, HD), jnp.bfloat16),
            jax.ShapeDtypeStruct((steps * TOPK // 32, BLK, BLK), jnp.int32),
        ],
        in_specs=[smem, smem] + [pl.BlockSpec(memory_space=pl.ANY)] * 2,
        out_specs=[pl.BlockSpec(memory_space=pl.ANY), pl.BlockSpec(memory_space=pltpu.VMEM)],
        scratch_shapes=[pltpu.SemaphoreType.DMA((4, CHUNKS)), pltpu.SemaphoreType.DMA((3, CHUNKS))],
        compiler_params=pltpu.CompilerParams(collective_id=0, has_side_effects=True, vmem_limit_bytes=16 << 20),
    )(chosen.reshape(-1), drop_seed, key, value)


def reduce_kernel(ranks, far_ref, own_ref, kg_ref, vg_ref, in_far, in_near, in_two, in_own, up_near, up_two,
                  in_head, up_head, total, send_sem, recv_sem, head_send, head_recv):
    shard = lax.axis_index("seq")
    rank = lax.axis_index("head")
    odd = lax.rem(shard, 2)
    mate = {"seq": shard + 1 - 2 * odd}
    back = seq_peer(-2)
    others = [{"head": lax.rem(rank + d, ranks)} for d in range(1, ranks)]
    meet([back, seq_peer(2), mate] + others)
    piece = in_near.shape[3]

    def rows(c):
        return pl.ds(c * piece, piece)

    def far_back(c):
        return remote(far_ref.at[2, :, :, rows(c)], in_far.at[c], send_sem.at[0, c], recv_sem.at[0, c], back)

    def own_mate(c):
        return remote(far_ref.at[0, :, :, rows(c)], in_own.at[c], send_sem.at[0, c], recv_sem.at[1, c], mate)

    def far_mate(c):
        return remote(far_ref.at[2, :, :, rows(c)], in_near.at[c], send_sem.at[1, c], recv_sem.at[2, c], mate)

    def near_mate(c):
        return remote(up_near.at[c], in_near.at[c], send_sem.at[1, c], recv_sem.at[2, c], mate)

    def two_back(c):
        return remote(up_two.at[c], in_two.at[c], send_sem.at[2, c], recv_sem.at[3, c], back)

    def to_head(c):
        return remote(up_head.at[c], in_head.at[rank], head_send.at[c], head_recv.at[rank], {"head": c})

    for c in range(ranks):
        @pl.when(odd == 0)
        def _():
            far_back(c).start()

        @pl.when(odd == 1)
        def _():
            far_mate(c).start()

    @pl.when(odd == 1)
    def _():
        for c in range(ranks):
            own_mate(c).start()

    def stage_near(c):
        @pl.when(odd == 0)
        def _():
            far_back(c).wait_recv()
            up_near[c] = (far_ref[0, :, :, rows(c)].astype(jnp.float32) + in_far[c].astype(jnp.float32)).astype(jnp.bfloat16)
            near_mate(c).start()

    def stage_two(c):
        near_mate(c).wait_recv()
        up_two[c] = (far_ref[1, :, :, rows(c)].astype(jnp.float32) + in_near[c].astype(jnp.float32)).astype(jnp.bfloat16)
        two_back(c).start()

    def stage_own(c):
        two_back(c).wait_recv()
        total[c] = own_ref[:, :, rows(c)] + in_two[c].astype(jnp.float32)

        @pl.when(odd == 0)
        def _():
            own_mate(c).wait_recv()
            total[c] += in_own[c].astype(jnp.float32)

        @pl.when(rank == c)
        def _():
            kg_ref[:, c * HD:(c + 1) * HD] = total[c, 0].T
            vg_ref[:, c * HD:(c + 1) * HD] = total[c, 1].T

        @pl.when(rank != c)
        def _():
            up_head[c] = total[c].astype(jnp.bfloat16)
            to_head(c).start()

    for k in range(ranks + 2):
        if k < ranks:
            stage_near(k)
        if 0 <= k - 1 < ranks:
            stage_two(k - 1)
        if 0 <= k - 2:
            stage_own(k - 2)

    for c in range(ranks):
        @pl.when(rank != c)
        def _():
            remote(up_head.at[c], in_head.at[c], head_send.at[c], head_recv.at[c], {"head": c}).wait_recv()
            kg_ref[:, c * HD:(c + 1) * HD] = in_head[c, 0].astype(jnp.float32).T
            vg_ref[:, c * HD:(c + 1) * HD] = in_head[c, 1].astype(jnp.float32).T
            to_head(c).wait_send()

        two_back(c).wait_send()

        @pl.when(odd == 0)
        def _():
            far_back(c).wait_send()
            near_mate(c).wait_send()

        @pl.when(odd == 1)
        def _():
            own_mate(c).wait_send()
            far_mate(c).wait_send()


def reduce(far, own):
    ranks = lax.axis_size("head")
    rows = own.shape[2]
    piece = rows // ranks
    part = pltpu.VMEM((ranks, 2, HD, piece), jnp.bfloat16)
    return pl.pallas_call(
        lambda *refs: reduce_kernel(ranks, *refs),
        name="reduce",
        out_shape=[jax.ShapeDtypeStruct((piece, ranks * HD), jnp.float32)] * 2,
        in_specs=[pl.BlockSpec(memory_space=pltpu.VMEM)] * 2,
        out_specs=[pl.BlockSpec(memory_space=pltpu.VMEM)] * 2,
        scratch_shapes=[part] * 8 + [
            pltpu.VMEM((ranks, 2, HD, piece), jnp.float32),
            pltpu.SemaphoreType.DMA((3, ranks)),
            pltpu.SemaphoreType.DMA((4, ranks)),
            pltpu.SemaphoreType.DMA((ranks,)),
            pltpu.SemaphoreType.DMA((ranks,)),
        ],
        compiler_params=pltpu.CompilerParams(collective_id=1, has_side_effects=True, vmem_limit_bytes=32 << 20),
    )(far, own)


def local(query, key, value, out_grad, chosen, drop_seed):
    rows = query.shape[0]
    local_heads = query.shape[1] // HD
    size = lax.axis_size("seq")
    ranks = lax.axis_size("head")
    window = min(SPAN, size // 2)
    kv_col = kv_column()
    paired = window == 4 and ranks == KVH and size % 2 == 0
    if paired:
        gathered, bits = gather(key, value, chosen, drop_seed)
    else:
        bits = masks(chosen, drop_seed, rows // BLK)
        own_pair = jnp.stack(
            [
                lax.dynamic_slice_in_dim(key, kv_col, HD, 1),
                lax.dynamic_slice_in_dim(value, kv_col, HD, 1),
            ]
        )
        gathered = jnp.stack([shifted(own_pair, "seq", d) for d in range(1, window)])
    query_grad, far, own = block_grads(query, out_grad, key, value, gathered, bits, chosen, drop_seed)
    if paired:
        key_grad, value_grad = reduce(far, own)
        return (query_grad, key_grad, value_grad)
    for d in range(1, window):
        own = own + shifted(far[d - 1], "seq", -d).astype(jnp.float32)
    pieces = own.transpose(0, 2, 1).reshape(2, ranks, rows // ranks, HD)
    swapped = lax.all_to_all(pieces, "head", 1, 1, tiled=True)
    summed = swapped.reshape(2, KVH, ranks // KVH, rows // ranks, HD).sum(2)
    both = summed.transpose(0, 2, 1, 3).reshape(2, rows // ranks, KVH * HD)
    return (query_grad, both[0], both[1])


def solution(mesh):
    in_specs = (
        P("seq", "head"),
        P("seq", None),
        P("seq", None),
        P("seq", "head"),
        P("head", "seq", None),
        P("head"),
    )
    out_specs = (P("seq", "head"), P(("seq", "head"), None), P(("seq", "head"), None))
    return jax.shard_map(local, mesh=mesh, in_specs=in_specs, out_specs=out_specs, check_vma=False)
```

time: 157 us -> 151 us (0.962)
  Pallas kernels: 149 us -> 140 us
  local copies, waits for them, and re-layouts: 5.59 us -> 10.7 us
    pallas_call x1, Pallas kernels: 91.1 us -> 80.6 us  [block_grads(): pl.pallas_call(kernel, name='block_grads', grid_spec=pltpu.PrefetchScalar...]
    unnamed x7 -> x19, local copies, waits for them, and re-layouts: 4.99 us -> 10.6 us
where the time goes in v1:
time: 151 us
  Pallas kernels  140 us (93%)
  local copies, waits for them, and re-layouts  10.7 us (7%)
    pallas_call x1, Pallas kernels, block_grads(): pl.pallas_call(kernel, name='block_grads', grid_spec=pltpu.PrefetchScalar...  80.6 us
    pallas_call x1, Pallas kernels, reduce(): pl.pallas_call(lambda *refs: reduce_kernel(ranks, *refs), name='reduce',...  34.1 us
    pallas_call x1, Pallas kernels, gather(): pl.pallas_call(lambda *refs: gather_kernel(steps, rows // BLK, *refs), na...  25 us
    unnamed x19, local copies, waits for them, and re-layouts  10.6 us

profile of v1, /device:TPU:23, one launch (start us, length us, event | category | flops | bytes accessed | tf_op | source)
XLA Modules:
  0.0 151.0 jit_solution(1539030348084553027)
XLA Ops:
  0.6 0.8 copy.10
  1.4 0.1 reshape.10.refs_0_
  1.5 0.0 copy-start.2
  1.5 1.2 copy-done.2
  2.7 0.0 copy-start.3
  2.7 1.2 copy-done.3
  4.0 0.0 copy-start.5
  4.0 0.7 copy-done.5
  4.6 0.0 copy-start.4
  4.6 25.0 %gather.1 = (bf16[3,2,1024,128]{3,2,1,0:T(8,128)(2,1)S(1)}, s32[2,512,512]{2,1,0:T(8,128)S(1)}) custom-call(s32[64]{0:T(128)S(1)} %reshape.10.refs_0_, s32[8]{0:T(128)S(1)} %copy-done.5, bf16[1024,512]{1,0:T(8,128)(2,1)S(1)} %copy-done.2, bf16[1024,512]{1,0:T(8,128)(2,1)S(1)} %copy-done.3), custom_call_target="tpu_custom_call" | custom-call | tf_op jit(solution)/shard_map/gather/pallas_call | solution.py:504
  29.6 0.0 copy-start.6
  29.6 1.3 copy-done.6
  30.9 0.0 copy-start.7
  30.9 1.2 copy-done.7
  32.1 0.0 copy-done.4
  32.1 80.6 %block_grads.1 = (f32[1024,1024]{1,0:T(8,128)}, bf16[3,2,128,1024]{3,2,1,0:T(8,128)(2,1)}, f32[2,128,1024]{2,1,0:T(8,128)}) custom-call(s32[64]{0:T(128)} %copy-done.4, s32[8]{0:T(128)} %refs_1_.3, bf16[1024,1024]{1,0:T(8,128)(2,1)} %refs_2_.3, bf16[1024,1024]{1,0:T(8,128)(2,1)} %refs_3_.3, bf16[1024,512]{1,0:T(8,128)(2,1)} %refs_4_.1, ...), custom_call_target="tpu_custom_call" | custom-call | flops 21474836480 | bytes 20971520 | tf_op jit(solution)/shard_map/block_grads/pallas_call | solution.py:282
  112.7 0.0 copy-start
  112.7 1.4 copy-done
  114.1 0.0 copy-start.1
  114.1 1.2 copy-done.1
  115.3 34.1 %reduce.1 = (f32[256,512]{1,0:T(8,128)S(1)}, f32[256,512]{1,0:T(8,128)S(1)}) custom-call(bf16[3,2,128,1024]{3,2,1,0:T(8,128)(2,1)S(1)} %copy-done, f32[2,128,1024]{2,1,0:T(8,128)S(1)} %copy-done.1), custom_call_target="tpu_custom_call" | custom-call | tf_op jit(solution)/shard_map/reduce/pallas_call | solution.py:629
  149.4 0.8 copy.13
  150.2 0.8 copy.14
Async XLA Ops:
  1.5 1.2 copy-start.2
  2.7 1.2 copy-start.3
  4.0 0.7 copy-start.5
  4.6 27.5 %copy-start.4 = (s32[64]{0:T(128)}, s32[64]{0:T(128)S(1)}, u32[]{:S(2)}) copy-start(s32[64]{0:T(128)S(1)} %reshape.10.refs_0_) | copy-start | bytes 772
  29.6 1.3 copy-start.6
  30.9 1.2 copy-start.7
  112.7 1.4 copy-start
  114.1 1.2 copy-start.1

commit v2 on v1

--- a/solution.py
+++ b/solution.py
@@ -15,6 +15,8 @@
 SPAN = 8
 SUB = 128
 ROWS = 16
+PIECE = 128
+LAG = 1
 
 drop_cut = 6554
 keep_gain = 1.0 / 0.9
@@ -65,6 +67,11 @@
     def low(t, row):
         return row // SUB * SUB if t == 0 else 0
 
+    def spread(x):
+        zero = jnp.maximum(jnp.minimum(x[-8:, :], 0.0), 0.0)
+        wide = zero.shape[1]
+        return jnp.concatenate([zero] * (BLK // wide) + ([zero[:, :BLK % wide]] if BLK % wide else []), axis=1)
+
     def score_parts(item, p):
         places = [place(pick) for pick in picks_of(item)]
 
@@ -78,6 +85,7 @@
             lo = low(t, row)
             keys = kv_ref[slot, 0, pl.ds(within + row, size), :]
             s = dot(keys, QT[p][:, lo:])
+            tie = spread(s)
             if t == 0:
                 edge = jnp.where(corner, s[:, :SUB], -jnp.inf)
                 s = edge if lo + SUB == BLK else jnp.concatenate([edge, s[:, SUB:]], axis=1)
@@ -86,22 +94,25 @@
             if row:
                 top = jnp.maximum(MX[p][t, :, lo:], top)
             MX[p][t, :, lo:] = top
+            return tie
 
         def pulls(t, row, size):
             slot, within = places[t]
             lo = low(t, row)
             values = kv_ref[slot, 1, pl.ds(within + row, size), :]
-            G[p][t * BLK + row:t * BLK + row + size, lo:] = dot(values, DT[p][:, lo:])
+            g = dot(values, DT[p][:, lo:])
+            G[p][t * BLK + row:t * BLK + row + size, lo:] = g
+            return spread(g)
 
         parts = [turn]
         for t in range(TOPK):
-            size = SUB if t == 0 else 2 * SUB
+            size = SUB if t == 0 else PIECE
             for row in range(0, BLK, size):
                 parts.append(lambda t=t, row=row, size=size: scores(t, row, size))
                 parts.append(lambda t=t, row=row, size=size: pulls(t, row, size))
         return parts
 
-    def soft_parts(item, p):
+    def soft_parts(item, p, ties):
         picks = picks_of(item)
         live = [None]
         for t in range(1, TOPK):
@@ -116,6 +127,7 @@
             for t in range(1, TOPK):
                 tops = jnp.maximum(tops, jnp.where(live[t], MX[p][t], -jnp.inf))
             peak = jnp.max(tops, axis=0, keepdims=True) * exp_scale
+            peak = jnp.broadcast_to(peak, (8, BLK))
             st["base"] = [peak] + [jnp.where(live[t], peak, 3e38) for t in range(1, TOPK)]
             st["total"] = jnp.zeros((8, BLK), jnp.float32)
             st["delta"] = jnp.zeros((8, BLK), jnp.float32)
@@ -127,13 +139,18 @@
             at = (slice(t * BLK + row, t * BLK + row + ROWS), slice(lo, BLK))
             bit = lax.shift_left(jnp.int32(1), lax.rem(item * TOPK, 32) + t)
             keep = (bits_ref[word, row:row + ROWS, lo:] & bit) != 0
-            e = jnp.exp2(S[p][at] * exp_scale - st["base"][t][:, lo:])
+            wide = BLK - lo
+            base = st["base"][t][:, lo:]
+            if ties:
+                base = base + ties.pop()[:, lo:]
+                st["base"][t] = base if not lo else jnp.concatenate([st["base"][t][:, :lo], base], axis=1)
+            scaled = (S[p][at] * exp_scale).reshape(ROWS // 8, 8, wide) - base[None]
+            e = jnp.exp2(scaled.reshape(ROWS, wide))
             d = jnp.where(keep, e, 0.0)
             dp = d * G[p][at]
             S[p][at] = e
             G[p][at] = dp
             D[p][at] = d.astype(jnp.bfloat16)
-            wide = BLK - lo
             e_sum = jnp.sum(e.reshape(ROWS // 8, 8, wide), axis=0)
             dp_sum = jnp.sum(dp.reshape(ROWS // 8, 8, wide), axis=0)
             if lo:
@@ -145,15 +162,19 @@
 
         def middle():
             inv = 1.0 / jnp.sum(st["total"], axis=0, keepdims=True)
-            st["mean"] = jnp.sum(st["delta"], axis=0, keepdims=True) * inv
+            st["mean"] = jnp.broadcast_to(jnp.sum(st["delta"], axis=0, keepdims=True) * inv, (8, BLK))
             INV[p][...] = inv
-            QN[p][...] = (QT[p][...].astype(jnp.float32) * inv).astype(jnp.bfloat16)
-            DN[p][...] = (DT[p][...].astype(jnp.float32) * inv).astype(jnp.bfloat16)
+            QN[p][...] = (QT[p][...].astype(jnp.float32) * inv).astype(jnp.bfloat16).T
+            DN[p][...] = (DT[p][...].astype(jnp.float32) * inv).astype(jnp.bfloat16).T
 
         def slope(t, row):
             lo = low(t, row)
             at = (slice(t * BLK + row, t * BLK + row + ROWS), slice(lo, BLK))
-            SG[p][at] = (G[p][at] - S[p][at] * st["mean"][:, lo:]).astype(jnp.bfloat16)
+            if ties:
+                st["mean"] = st["mean"] + ties.pop()
+            wide = BLK - lo
+            less = S[p][at].reshape(ROWS // 8, 8, wide) * st["mean"][None, :, lo:]
+            SG[p][at] = (G[p][at] - less.reshape(ROWS, wide)).astype(jnp.bfloat16)
 
         parts = [(1, head)]
         spots = [(t, row) for t in range(TOPK) for row in range(0, BLK, ROWS)]
@@ -167,22 +188,26 @@
     def grad_parts(item, p):
         places = [place(pick) for pick in picks_of(item)]
 
-        def keyed(t, part):
+        def keyed(t, part, row, size):
             slot, within = places[t]
-            left, right = ((QN, SG), (DN, D))[part]
-            add = lax.dot_general(left[p][...], right[p][t * BLK:(t + 1) * BLK, :], (((1,), (1,)), ((), ())),
-                                  preferred_element_type=jnp.float32)
-            acc_ref[slot, part, :, pl.ds(within, BLK)] += add
+            left, right = ((SG, QN), (D, DN))[part]
+            start = t * BLK + row
+            wide = low(t, row) if size <= SUB else 0
+            add = dot(left[p][start:start + size, wide:], right[p][wide:, :])
+            acc_ref[slot, part, pl.ds(within + row, size), :] += add
+            return spread(add)
 
         def queried(lo, size):
             keys_t = jnp.concatenate([kt_ref[slot, :, pl.ds(within, BLK)] for slot, within in places], axis=1)
             part = dot(keys_t, SG[p][:, lo:lo + size])
             OUT[p][lo:lo + size, :] = (part * (INV[p][:, lo:lo + size] * (keep_gain * factor))).T
+            return spread(part)
 
         parts = []
         for t in range(TOPK):
-            parts.append(lambda t=t: keyed(t, 1))
-            parts.append(lambda t=t: keyed(t, 0))
+            for row in range(0, BLK, PIECE):
+                parts.append(lambda t=t, row=row: keyed(t, 1, row, PIECE))
+                parts.append(lambda t=t, row=row: keyed(t, 0, row, PIECE))
             if t % 2:
                 parts.append(lambda t=t: queried(t // 2 * 2 * SUB, 2 * SUB))
         return parts
@@ -191,13 +216,18 @@
         for part in parts:
             part()
 
-    def mix(soft, dots):
+    def mix(soft, dots, ties):
         whole = sum(cost for cost, _ in soft)
         done, k = 0, 0
+        held = []
         for cost, part in soft:
             while k < len(dots) and k * whole <= done * len(dots):
-                dots[k]()
+                held.append(dots[k]())
                 k += 1
+                if len(held) > LAG:
+                    tie = held.pop(0)
+                    if tie is not None:
+                        ties[:] = [tie if not ties else ties[0] + tie]
             part()
             done += cost
         run(dots[k:])
@@ -247,9 +277,8 @@
         def _():
             send(jnp.maximum(target - 2, 0), 1 - p).wait()
 
-        if p == 1:
-            pass
-        mix(soft_parts(item, p), weave(score_parts(after, 1 - p), grad_parts(before, 1 - p)))
+        ties = []
+        mix(soft_parts(item, p, ties), weave(score_parts(after, 1 - p), grad_parts(before, 1 - p)), ties)
         send(target, 1 - p).start()
 
     @pl.when(pair == last)
@@ -288,16 +317,16 @@
             in_specs=[pl.BlockSpec(memory_space=pl.ANY)] * 6,
             out_specs=[
                 pl.BlockSpec(memory_space=pl.ANY),
-                pl.BlockSpec((window - 1, 2, HD, rows), lambda i, *_: (0, 0, 0, 0)),
-                pl.BlockSpec((2, HD, rows), lambda i, *_: (0, 0, 0)),
+                pl.BlockSpec((window - 1, 2, rows, HD), lambda i, *_: (0, 0, 0, 0)),
+                pl.BlockSpec((2, rows, HD), lambda i, *_: (0, 0, 0)),
             ],
             scratch_shapes=twice((TOPK * BLK, BLK), f32) + twice((TOPK * BLK, BLK), f32)
             + twice((TOPK * BLK, BLK), bf16) + twice((TOPK * BLK, BLK), bf16)
             + twice((TOPK, 8, BLK), f32)
-            + twice((HD, BLK), bf16) * 4
+            + twice((HD, BLK), bf16) * 2 + twice((BLK, HD), bf16) * 2
             + twice((1, BLK), f32) + twice((BLK, HD), f32)
             + [
-                pltpu.VMEM((window, 2, HD, rows), f32),
+                pltpu.VMEM((window, 2, rows, HD), f32),
                 pltpu.VMEM((window, HD, rows), bf16),
                 pltpu.VMEM((window, 2, rows, HD), bf16),
                 pltpu.VMEM(bits.shape, jnp.int32),
@@ -309,8 +338,8 @@
         ),
         out_shape=[
             jax.ShapeDtypeStruct((rows, local_heads * HD), f32),
-            jax.ShapeDtypeStruct((window - 1, 2, HD, rows), bf16),
-            jax.ShapeDtypeStruct((2, HD, rows), f32),
+            jax.ShapeDtypeStruct((window - 1, 2, rows, HD), bf16),
+            jax.ShapeDtypeStruct((2, rows, HD), f32),
         ],
         compiler_params=pltpu.CompilerParams(vmem_limit_bytes=60 << 20),
         cost_estimate=pl.CostEstimate(flops=flops, bytes_accessed=20 << 20, transcendentals=steps * TOPK * BLK * BLK),
@@ -511,32 +540,38 @@
         in_specs=[smem, smem] + [pl.BlockSpec(memory_space=pl.ANY)] * 2,
         out_specs=[pl.BlockSpec(memory_space=pl.ANY), pl.BlockSpec(memory_space=pltpu.VMEM)],
         scratch_shapes=[pltpu.SemaphoreType.DMA((4, CHUNKS)), pltpu.SemaphoreType.DMA((3, CHUNKS))],
-        compiler_params=pltpu.CompilerParams(collective_id=0, has_side_effects=True, vmem_limit_bytes=16 << 20),
+        compiler_params=pltpu.CompilerParams(collective_id=0, has_side_effects=True, vmem_limit_bytes=60 << 20),
     )(chosen.reshape(-1), drop_seed, key, value)
 
 
-def reduce_kernel(ranks, far_ref, own_ref, kg_ref, vg_ref, in_far, in_near, in_two, in_own, up_near, up_two,
-                  in_head, up_head, total, send_sem, recv_sem, head_send, head_recv):
+def reduce_kernel(ranks, far_hbm, own_hbm, kg_ref, vg_ref, in_far, in_near, in_two, in_own, up_near, up_two,
+                  in_head, up_head, total, far_ref, own_ref, send_sem, recv_sem, head_send, head_recv, load_sem):
     shard = lax.axis_index("seq")
     rank = lax.axis_index("head")
     odd = lax.rem(shard, 2)
     mate = {"seq": shard + 1 - 2 * odd}
     back = seq_peer(-2)
     others = [{"head": lax.rem(rank + d, ranks)} for d in range(1, ranks)]
+    loads = [
+        pltpu.make_async_copy(far_hbm.at[pl.ds(0, 2)], far_ref, load_sem.at[0]),
+        pltpu.make_async_copy(own_hbm, own_ref, load_sem.at[1]),
+    ]
+    for load in loads:
+        load.start()
     meet([back, seq_peer(2), mate] + others)
-    piece = in_near.shape[3]
+    piece = in_near.shape[2]
 
     def rows(c):
         return pl.ds(c * piece, piece)
 
     def far_back(c):
-        return remote(far_ref.at[2, :, :, rows(c)], in_far.at[c], send_sem.at[0, c], recv_sem.at[0, c], back)
+        return remote(far_hbm.at[2, :, rows(c)], in_far.at[c], send_sem.at[0, c], recv_sem.at[0, c], back)
 
     def own_mate(c):
-        return remote(far_ref.at[0, :, :, rows(c)], in_own.at[c], send_sem.at[0, c], recv_sem.at[1, c], mate)
+        return remote(far_hbm.at[0, :, rows(c)], in_own.at[c], send_sem.at[0, c], recv_sem.at[1, c], mate)
 
     def far_mate(c):
-        return remote(far_ref.at[2, :, :, rows(c)], in_near.at[c], send_sem.at[1, c], recv_sem.at[2, c], mate)
+        return remote(far_hbm.at[2, :, rows(c)], in_near.at[c], send_sem.at[1, c], recv_sem.at[2, c], mate)
 
     def near_mate(c):
         return remote(up_near.at[c], in_near.at[c], send_sem.at[1, c], recv_sem.at[2, c], mate)
@@ -565,17 +600,17 @@
         @pl.when(odd == 0)
         def _():
             far_back(c).wait_recv()
-            up_near[c] = (far_ref[0, :, :, rows(c)].astype(jnp.float32) + in_far[c].astype(jnp.float32)).astype(jnp.bfloat16)
+            up_near[c] = (far_ref[0, :, rows(c)].astype(jnp.float32) + in_far[c].astype(jnp.float32)).astype(jnp.bfloat16)
             near_mate(c).start()
 
     def stage_two(c):
         near_mate(c).wait_recv()
-        up_two[c] = (far_ref[1, :, :, rows(c)].astype(jnp.float32) + in_near[c].astype(jnp.float32)).astype(jnp.bfloat16)
+        up_two[c] = (far_ref[1, :, rows(c)].astype(jnp.float32) + in_near[c].astype(jnp.float32)).astype(jnp.bfloat16)
         two_back(c).start()
 
     def stage_own(c):
         two_back(c).wait_recv()
-        total[c] = own_ref[:, :, rows(c)] + in_two[c].astype(jnp.float32)
+        total[c] = own_ref[:, rows(c)] + in_two[c].astype(jnp.float32)
 
         @pl.when(odd == 0)
         def _():
@@ -584,14 +619,16 @@
 
         @pl.when(rank == c)
         def _():
-            kg_ref[:, c * HD:(c + 1) * HD] = total[c, 0].T
-            vg_ref[:, c * HD:(c + 1) * HD] = total[c, 1].T
+            kg_ref[:, c * HD:(c + 1) * HD] = total[c, 0]
+            vg_ref[:, c * HD:(c + 1) * HD] = total[c, 1]
 
         @pl.when(rank != c)
         def _():
             up_head[c] = total[c].astype(jnp.bfloat16)
             to_head(c).start()
 
+    for load in loads:
+        load.wait()
     for k in range(ranks + 2):
         if k < ranks:
             stage_near(k)
@@ -604,8 +641,8 @@
         @pl.when(rank != c)
         def _():
             remote(up_head.at[c], in_head.at[c], head_send.at[c], head_recv.at[c], {"head": c}).wait_recv()
-            kg_ref[:, c * HD:(c + 1) * HD] = in_head[c, 0].astype(jnp.float32).T
-            vg_ref[:, c * HD:(c + 1) * HD] = in_head[c, 1].astype(jnp.float32).T
+            kg_ref[:, c * HD:(c + 1) * HD] = in_head[c, 0].astype(jnp.float32)
+            vg_ref[:, c * HD:(c + 1) * HD] = in_head[c, 1].astype(jnp.float32)
             to_head(c).wait_send()
 
         two_back(c).wait_send()
@@ -623,23 +660,26 @@
 
 def reduce(far, own):
     ranks = lax.axis_size("head")
-    rows = own.shape[2]
+    rows = own.shape[1]
     piece = rows // ranks
-    part = pltpu.VMEM((ranks, 2, HD, piece), jnp.bfloat16)
+    part = pltpu.VMEM((ranks, 2, piece, HD), jnp.bfloat16)
     return pl.pallas_call(
         lambda *refs: reduce_kernel(ranks, *refs),
         name="reduce",
         out_shape=[jax.ShapeDtypeStruct((piece, ranks * HD), jnp.float32)] * 2,
-        in_specs=[pl.BlockSpec(memory_space=pltpu.VMEM)] * 2,
+        in_specs=[pl.BlockSpec(memory_space=pl.ANY)] * 2,
         out_specs=[pl.BlockSpec(memory_space=pltpu.VMEM)] * 2,
         scratch_shapes=[part] * 8 + [
-            pltpu.VMEM((ranks, 2, HD, piece), jnp.float32),
+            pltpu.VMEM((ranks, 2, piece, HD), jnp.float32),
+            pltpu.VMEM((2,) + far.shape[1:], jnp.bfloat16),
+            pltpu.VMEM(own.shape, jnp.float32),
             pltpu.SemaphoreType.DMA((3, ranks)),
             pltpu.SemaphoreType.DMA((4, ranks)),
             pltpu.SemaphoreType.DMA((ranks,)),
             pltpu.SemaphoreType.DMA((ranks,)),
+            pltpu.SemaphoreType.DMA((2,)),
         ],
-        compiler_params=pltpu.CompilerParams(collective_id=1, has_side_effects=True, vmem_limit_bytes=32 << 20),
+        compiler_params=pltpu.CompilerParams(collective_id=1, has_side_effects=True, vmem_limit_bytes=60 << 20),
     )(far, own)
 
 
@@ -668,7 +708,7 @@
         return (query_grad, key_grad, value_grad)
     for d in range(1, window):
         own = own + shifted(far[d - 1], "seq", -d).astype(jnp.float32)
-    pieces = own.transpose(0, 2, 1).reshape(2, ranks, rows // ranks, HD)
+    pieces = own.reshape(2, ranks, rows // ranks, HD)
     swapped = lax.all_to_all(pieces, "head", 1, 1, tiled=True)
     summed = swapped.reshape(2, KVH, ranks // KVH, rows // ranks, HD).sum(2)
     both = summed.transpose(0, 2, 1, 3).reshape(2, rows // ranks, KVH * HD)

time: 151 us -> 140 us (0.927)
  Pallas kernels: 140 us -> 134 us
  local copies, waits for them, and re-layouts: 10.7 us -> 5.12 us
    pallas_call x1, Pallas kernels: 80.6 us -> 72.2 us  [block_grads(): pl.pallas_call(kernel, name='block_grads', grid_spec=pltpu.PrefetchScalar...]
    unnamed x19 -> x3, local copies, waits for them, and re-layouts: 10.6 us -> 4.51 us
    pallas_call x1, Pallas kernels: 25 us -> 26.8 us  [gather(): pl.pallas_call(lambda *refs: gather_kernel(steps, rows // BLK, *refs), na...]
where the time goes in v2:
time: 140 us
  Pallas kernels  134 us (96%)
  local copies, waits for them, and re-layouts  5.12 us (4%)
    pallas_call x1, Pallas kernels, block_grads(): pl.pallas_call(kernel, name='block_grads', grid_spec=pltpu.PrefetchScalar...  72.2 us
    pallas_call x1, Pallas kernels, reduce(): pl.pallas_call(lambda *refs: reduce_kernel(ranks, *refs), name='reduce',...  35.3 us
    pallas_call x1, Pallas kernels, gather(): pl.pallas_call(lambda *refs: gather_kernel(steps, rows // BLK, *refs), na...  26.8 us
    unnamed x3, local copies, waits for them, and re-layouts  4.51 us

profile of v2, /device:TPU:23, one launch (start us, length us, event | category | flops | bytes accessed | tf_op | source)
XLA Modules:
  0.0 140.0 jit_solution(16881555552585496340)
XLA Ops:
  0.6 0.8 copy.10
  1.4 0.6 reshape.10.refs_0_
  2.0 26.8 %gather.1 = (bf16[3,2,1024,128]{3,2,1,0:T(8,128)(2,1)}, s32[2,512,512]{2,1,0:T(8,128)}) custom-call(s32[64]{0:T(128)} %reshape.10.refs_0_, s32[8]{0:T(128)} %refs_1_.3, bf16[1024,512]{1,0:T(8,128)(2,1)} %refs_4_.1, bf16[1024,512]{1,0:T(8,128)(2,1)} %refs_5_.1), custom_call_target="tpu_custom_call" | custom-call | tf_op jit(solution)/shard_map/gather/pallas_call | solution.py:533
  28.8 72.2 %block_grads.1 = (f32[1024,1024]{1,0:T(8,128)}, bf16[3,2,1024,128]{3,2,1,0:T(8,128)(2,1)}, f32[2,1024,128]{2,1,0:T(8,128)}) custom-call(s32[64]{0:T(128)} %reshape.10.refs_0_, s32[8]{0:T(128)} %refs_1_.3, bf16[1024,1024]{1,0:T(8,128)(2,1)} %refs_2_.3, bf16[1024,1024]{1,0:T(8,128)(2,1)} %refs_3_.3, bf16[1024,512]{1,0:T(8,128)(2,1)} %refs_4_.1, ...), custom_call_target="tpu_custom_call" | custom-call | flops 21474836480 | bytes 20971520 | tf_op jit(solution)/shard_map/block_grads/pallas_call | solution.py:311
  101.0 35.3 %reduce.1 = (f32[256,512]{1,0:T(8,128)}, f32[256,512]{1,0:T(8,128)}) custom-call(bf16[3,2,1024,128]{3,2,1,0:T(8,128)(2,1)} %get-tuple-element.13.refs_0_, f32[2,1024,128]{2,1,0:T(8,128)} %get-tuple-element.14.refs_1_), custom_call_target="tpu_custom_call" | custom-call | tf_op jit(solution)/shard_map/reduce/pallas_call | solution.py:666
  136.3 1.9 %copy.13 = f32[256,512]{1,0:T(8,128)} copy(f32[256,512]{1,0:T(8,128)} %get-tuple-element.21) | data formatting | bytes 1048576
  138.2 1.9 %copy.14 = f32[256,512]{1,0:T(8,128)} copy(f32[256,512]{1,0:T(8,128)} %get-tuple-element.22) | data formatting | bytes 1048576
